TPU v7x, 256 devices: a whole 4x4x8 slice. The times are simulated.
256 devices in a mesh: dom: 64 (over x, z, core), slab: 4 (over y).
Axes of the slice: x: 4, y: 4, z: 8, core: 2. Of those that a mesh axis runs over, the one named last changes fastest.
Arguments:
- logperm: float32 [256, 16, 64, 128], P('dom', 'slab'), may hold values from -4.2 to 4.2
- source: float32 [16, 64, 128], P('slab'), may hold values from -6 to 6
- observed: float32 [16, 64, 128], P('slab'), may hold values from -1.2 to 1.2
- brownian: float32 [256, 256], replicated, may hold values from -6 to 6
Outputs:
- particles_next: float32 [256, 16, 64, 128], P('dom', 'slab')
All inputs are finite; a program needn't handle non-finite values.
Results may differ from a plain program's by a relative error of at most 0.0003.
Values sent between devices are 32-bit elements; how exact they have to be, the bound alone decides.
No kernel may reach another device: no remote copies, remote signals or barrier semaphores. Data moves between devices by JAX's collectives and lax.ppermute only.
A program may use at most 64 MiB of HBM per device.

v0:
```python
import math
import jax
import jax.numpy as jnp
from jax import lax
from jax.sharding import PartitionSpec as P

SWEEPS = 8
misfit_weight = 1000.0


def with_halo(block, sides, width):
    for axis, dim in sides:
        count = lax.axis_size(axis)
        forward = [(i, i + 1) for i in range(count - 1)]
        backward = [(target, source) for source, target in forward]
        low = lax.ppermute(
            lax.slice_in_dim(block, block.shape[dim] - width, None, axis=dim), axis, forward
        )
        high = lax.ppermute(lax.slice_in_dim(block, 0, width, axis=dim), axis, backward)
        block = jnp.concatenate([low, block, high], axis=dim)
    return block


def neighbor_sum(core, below, above, fill):
    pad_y = jnp.pad(core, ((0, 0), (0, 0), (1, 1), (0, 0)), constant_values=fill)
    pad_z = jnp.pad(core, ((0, 0), (0, 0), (0, 0), (1, 1)), constant_values=fill)
    return below + above + pad_y[:, :, :-2] + pad_y[:, :, 2:] + pad_z[..., :-2] + pad_z[..., 2:]


def grad_field(e_core, e_below, e_above, p_core, p_below, p_above, q_core, q_below, q_above):
    summed = e_below * (p_core - p_below) * (q_core - q_below) + e_above * (p_core - p_above) * (
        q_core - q_above
    )
    for dimension in (2, 3):
        padding = [(0, 0), (0, 0), (0, 0), (0, 0)]
        padding[dimension] = (1, 1)
        e_pad = jnp.pad(e_core, padding, constant_values=1.0)
        p_pad = jnp.pad(p_core, padding)
        q_pad = jnp.pad(q_core, padding)
        extent = e_core.shape[dimension]
        for offset in (0, 2):
            e_near = lax.slice_in_dim(e_pad, offset, offset + extent, axis=dimension)
            p_near = lax.slice_in_dim(p_pad, offset, offset + extent, axis=dimension)
            q_near = lax.slice_in_dim(q_pad, offset, offset + extent, axis=dimension)
            summed = summed + e_near * (p_core - p_near) * (q_core - q_near)
    return -0.5 * e_core * summed


def on_device(logperm, source, observed, brownian):
    particles, width, rows_y, depth_z = logperm.shape
    slabs = lax.axis_size("slab")
    cells = width * slabs * rows_y * depth_z
    extended = with_halo(logperm, (("slab", 1),), 1)
    e_ext = jnp.exp(0.5 * extended)
    e_core = e_ext[:, 1:-1]
    inverse = 1.0 / neighbor_sum(e_core, e_ext[:, :-2], e_ext[:, 2:], 1.0)

    def relax_rim(rhs):
        value = inverse * rhs
        for sweep_index in range(SWEEPS - 1):
            bordered = with_halo(value, (("slab", 1),), 1)
            value = inverse * (
                rhs + e_core * neighbor_sum(value, bordered[:, :-2], bordered[:, 2:], 0.0)
            )
        return value / e_core

    pressure = relax_rim(source[None])
    misfit = misfit_weight * (pressure - observed[None])
    adjoint = relax_rim(misfit)
    states = with_halo(jnp.stack([pressure, adjoint]), (("slab", 2),), 1)
    gradient = grad_field(
        e_core,
        e_ext[:, :-2],
        e_ext[:, 2:],
        pressure,
        states[0][:, :-2],
        states[0][:, 2:],
        adjoint,
        states[1][:, :-2],
        states[1][:, 2:],
    )
    g_flat = gradient.reshape(particles, -1)
    u_cells, g_cells = (
        lax.all_to_all(
            logperm.reshape(particles, -1), "dom", split_axis=1, concat_axis=0, tiled=True
        ),
        lax.all_to_all(g_flat, "dom", split_axis=1, concat_axis=0, tiled=True),
    )
    ensemble = u_cells.shape[0]
    centre = jnp.mean(u_cells, axis=0, keepdims=True)
    spread = u_cells - centre
    partial_gram = lax.dot_general(
        spread,
        g_cells,
        (((1,), (1,)), ((), ())),
        precision=lax.Precision.HIGHEST,
        preferred_element_type=jnp.float32,
    )
    gram = lax.psum(partial_gram, ("dom", "slab"))
    step_size = ensemble / (4.0 * (cells + 1))
    mixing = -(step_size / ensemble) * gram + math.sqrt(2.0 * step_size / ensemble) * brownian
    moved = (
        centre
        + 1.25 * spread
        + lax.dot_general(
            mixing,
            spread,
            (((0,), (0,)), ((), ())),
            precision=lax.Precision.HIGHEST,
            preferred_element_type=jnp.float32,
        )
    )
    returned = lax.all_to_all(moved, "dom", split_axis=0, concat_axis=1, tiled=True)
    return returned.reshape(logperm.shape)


def solution(mesh):
    return jax.shard_map(
        on_device,
        mesh=mesh,
        in_specs=(P("dom", "slab", None, None), P("slab", None, None), P("slab", None, None), P()),
        out_specs=P("dom", "slab", None, None),
        check_vma=False,
    )
```

profile of v0, /device:TPU:1, one launch (start us, length us, event | category | flops | bytes accessed | tf_op | source)
XLA Modules:
  0.0 498.0 jit_solution(12891519340523834035)
XLA Ops:
  7.6 4.0 collective-permute-start
  13.7 3.6 collective-permute-done.1
  18.9 3.2 collective-permute-start.2
  24.1 3.8 collective-permute-done.3
  28.3 2.9 collective-permute-start.4
  33.1 3.8 collective-permute-done.5
  37.3 2.2 collective-permute-start.6
  41.5 3.8 collective-permute-done.7
  49.5 3.8 collective-permute-done.9
  57.6 3.8 collective-permute-done.11
  61.8 2.1 collective-permute-start.12
  66.1 4.1 collective-permute-done.13
  75.3 3.9 collective-permute-done.15
  79.7 2.1 collective-permute-start.16
  84.2 3.8 collective-permute-done.17
  88.4 2.2 collective-permute-start.18
  92.6 3.8 collective-permute-done.19
  96.9 2.2 collective-permute-start.20
  101.0 3.8 collective-permute-done.21
  105.3 2.2 collective-permute-start.22
  109.4 3.8 collective-permute-done.23
  113.7 1.9 collective-permute-start.24
  117.5 3.8 collective-permute-done.25
  125.7 3.8 collective-permute-done.27
  133.8 3.9 collective-permute-done.29
  139.1 2.6 collective-permute-start.30
  144.2 28.9 %all-to-all-start = ((f32[4,64,512]{2,0,1:T(4,128)}), f32[4,64,512]{2,0,1:T(4,128)S(1)}, u32[]{:S(2)}, u32[]{:S(2)}) async-start(f32[4,64,512]{2,0,1:T(4,128)} %copy.7), calls=%async_computation | async-start | bytes 1048576 | tf_op jit(solution)/shard_map/all_to_all | solution.py:84
  176.8 13.7 %all-to-all-done = f32[4,64,512]{2,0,1:T(4,128)S(1)} async-done(((f32[4,64,512]{2,0,1:T(4,128)}), f32[4,64,512]{2,0,1:T(4,128)S(1)}, u32[]{:S(2)}, u32[]{:S(2)}) %all-to-all-start) | async-done | bytes 524320 | tf_op jit(solution)/shard_map/all_to_all | solution.py:84
  190.4 6.3 %all-to-all-start.1 = ((f32[4,64,512]{2,0,1:T(4,128)}), f32[4,64,512]{2,0,1:T(4,128)S(1)}, u32[]{:S(2)}, u32[]{:S(2)}) async-start(f32[4,64,512]{2,0,1:T(4,128)} %copy.8), calls=%async_computation.1 | async-start | bytes 1048576 | tf_op jit(solution)/shard_map/all_to_all | solution.py:87
  197.2 16.9 %all-to-all-done.1 = f32[4,64,512]{2,0,1:T(4,128)S(1)} async-done(((f32[4,64,512]{2,0,1:T(4,128)}), f32[4,64,512]{2,0,1:T(4,128)S(1)}, u32[]{:S(2)}, u32[]{:S(2)}) %all-to-all-start.1) | async-done | bytes 524320 | tf_op jit(solution)/shard_map/all_to_all | solution.py:87
  215.8 245.4 %all-reduce.36.cloned.1.call-done = f32[256,256]{1,0:T(8,128)} async-done(((f32[256,256]{1,0:T(8,128)}), f32[256,256]{1,0:T(8,128)}) %all-reduce.36.cloned.1.call-update) | async-done | bytes 262160 | tf_op jit(solution)/shard_map/psum | solution.py:99
  462.9 27.3 %all_to_all.54 = f32[64,4,512]{2,1,0:T(4,128)S(1)} all-to-all(f32[64,4,512]{2,1,0:T(4,128)S(1)} %all_to_all.48), channel_id=1, replica_groups=mesh['dom'=64,'slab'=4] {'dom'}, dimensions={0} | all-to-all | bytes 1048576 | tf_op jit(solution)/shard_map/all_to_all | solution.py:113
  (99 shorter events, 60.8 us)
Async XLA Ops:
  7.6 6.2 %collective-permute-start = (f32[4,1,64,128]{3,2,1,0:T(8,128)S(1)}, f32[4,1,64,128]{3,2,1,0:T(8,128)S(1)}, u32[]{:S(2)}, u32[]{:S(2)}) collective-permute-start(f32[4,1,64,128]{3,2,1,0:T(8,128)S(1)} %get-tuple-element.41), channel_id=1, source_target_pairs={{0,1},{1,2},{2,3},{4,5},{5,6},{6,7},{8,9},{9,10},{10,11},{12,13},{... | collective-permute-start | bytes 393224 | tf_op jit(solution)/shard_map/ppermute | solution.py:16
  11.6 5.7 %collective-permute-start.1 = (f32[4,1,64,128]{3,2,1,0:T(8,128)S(1)}, f32[4,1,64,128]{3,2,1,0:T(8,128)S(1)}, u32[]{:S(2)}, u32[]{:S(2)}) collective-permute-start(f32[4,1,64,128]{3,2,1,0:T(8,128)S(1)} %get-tuple-element.42), channel_id=1, source_target_pairs={{1,0},{2,1},{3,2},{5,4},{6,5},{7,6},{9,8},{10,9},{11,10},{13,12},{... | collective-permute-start | bytes 393224 | tf_op jit(solution)/shard_map/ppermute | solution.py:19
  18.9 5.1 %collective-permute-start.2 = (f32[4,1,64,128]{3,2,1,0:T(8,128)S(1)}, f32[4,1,64,128]{3,2,1,0:T(8,128)S(1)}, u32[]{:S(2)}, u32[]{:S(2)}) collective-permute-start(f32[4,1,64,128]{3,2,1,0:T(8,128)S(1)} %get-tuple-element.39), channel_id=1, source_target_pairs={{0,1},{1,2},{2,3},{4,5},{5,6},{6,7},{8,9},{9,10},{10,11},{12,13},{... | collective-permute-start | bytes 393224 | tf_op jit(solution)/shard_map/ppermute | solution.py:16
  22.2 5.7 %collective-permute-start.3 = (f32[4,1,64,128]{3,2,1,0:T(8,128)S(1)}, f32[4,1,64,128]{3,2,1,0:T(8,128)S(1)}, u32[]{:S(2)}, u32[]{:S(2)}) collective-permute-start(f32[4,1,64,128]{3,2,1,0:T(8,128)S(1)} %get-tuple-element.40), channel_id=1, source_target_pairs={{1,0},{2,1},{3,2},{5,4},{6,5},{7,6},{9,8},{10,9},{11,10},{13,12},{... | collective-permute-start | bytes 393224 | tf_op jit(solution)/shard_map/ppermute | solution.py:19
  28.3 4.8 collective-permute-start.4
  31.2 5.7 %collective-permute-start.5 = (f32[4,1,64,128]{3,2,1,0:T(8,128)S(1)}, f32[4,1,64,128]{3,2,1,0:T(8,128)S(1)}, u32[]{:S(2)}, u32[]{:S(2)}) collective-permute-start(f32[4,1,64,128]{3,2,1,0:T(8,128)S(1)} %get-tuple-element.38), channel_id=1, source_target_pairs={{1,0},{2,1},{3,2},{5,4},{6,5},{7,6},{9,8},{10,9},{11,10},{13,12},{... | collective-permute-start | bytes 393224 | tf_op jit(solution)/shard_map/ppermute | solution.py:19
  37.3 4.1 collective-permute-start.6
  39.6 5.7 %collective-permute-start.7 = (f32[4,1,64,128]{3,2,1,0:T(8,128)S(1)}, f32[4,1,64,128]{3,2,1,0:T(8,128)S(1)}, u32[]{:S(2)}, u32[]{:S(2)}) collective-permute-start(f32[4,1,64,128]{3,2,1,0:T(8,128)S(1)} %get-tuple-element.36), channel_id=1, source_target_pairs={{1,0},{2,1},{3,2},{5,4},{6,5},{7,6},{9,8},{10,9},{11,10},{13,12},{... | collective-permute-start | bytes 393224 | tf_op jit(solution)/shard_map/ppermute | solution.py:19
  47.6 5.7 %collective-permute-start.9 = (f32[4,1,64,128]{3,2,1,0:T(8,128)S(1)}, f32[4,1,64,128]{3,2,1,0:T(8,128)S(1)}, u32[]{:S(2)}, u32[]{:S(2)}) collective-permute-start(f32[4,1,64,128]{3,2,1,0:T(8,128)S(1)} %get-tuple-element.34), channel_id=1, source_target_pairs={{1,0},{2,1},{3,2},{5,4},{6,5},{7,6},{9,8},{10,9},{11,10},{13,12},{... | collective-permute-start | bytes 393224 | tf_op jit(solution)/shard_map/ppermute | solution.py:19
  53.7 3.9 collective-permute-start.10
  55.7 5.7 %collective-permute-start.11 = (f32[4,1,64,128]{3,2,1,0:T(8,128)S(1)}, f32[4,1,64,128]{3,2,1,0:T(8,128)S(1)}, u32[]{:S(2)}, u32[]{:S(2)}) collective-permute-start(f32[4,1,64,128]{3,2,1,0:T(8,128)S(1)} %get-tuple-element.32), channel_id=1, source_target_pairs={{1,0},{2,1},{3,2},{5,4},{6,5},{7,6},{9,8},{10,9},{11,10},{13,12},{... | collective-permute-start | bytes 393224 | tf_op jit(solution)/shard_map/ppermute | solution.py:19
  61.8 4.3 collective-permute-start.12
  63.9 6.3 %collective-permute-start.13 = (f32[4,1,64,128]{3,2,1,0:T(8,128)S(1)}, f32[4,1,64,128]{3,2,1,0:T(8,128)S(1)}, u32[]{:S(2)}, u32[]{:S(2)}) collective-permute-start(f32[4,1,64,128]{3,2,1,0:T(8,128)S(1)} %get-tuple-element.30), channel_id=1, source_target_pairs={{1,0},{2,1},{3,2},{5,4},{6,5},{7,6},{9,8},{10,9},{11,10},{13,12},{... | collective-permute-start | bytes 393224 | tf_op jit(solution)/shard_map/ppermute | solution.py:19
  70.6 4.7 collective-permute-start.14
  72.3 7.0 %collective-permute-start.15 = (f32[4,1,64,128]{3,2,1,0:T(8,128)S(1)}, f32[4,1,64,128]{3,2,1,0:T(8,128)S(1)}, u32[]{:S(2)}, u32[]{:S(2)}) collective-permute-start(f32[4,1,64,128]{3,2,1,0:T(8,128)S(1)} %get-tuple-element.28), channel_id=1, source_target_pairs={{1,0},{2,1},{3,2},{5,4},{6,5},{7,6},{9,8},{10,9},{11,10},{13,12},{... | collective-permute-start | bytes 393224 | tf_op jit(solution)/shard_map/ppermute | solution.py:19
  79.7 4.4 collective-permute-start.16
  81.9 6.1 %collective-permute-start.17 = (f32[4,1,64,128]{3,2,1,0:T(8,128)S(1)}, f32[4,1,64,128]{3,2,1,0:T(8,128)S(1)}, u32[]{:S(2)}, u32[]{:S(2)}) collective-permute-start(f32[4,1,64,128]{3,2,1,0:T(8,128)S(1)} %get-tuple-element.26), channel_id=1, source_target_pairs={{1,0},{2,1},{3,2},{5,4},{6,5},{7,6},{9,8},{10,9},{11,10},{13,12},{... | collective-permute-start | bytes 393224 | tf_op jit(solution)/shard_map/ppermute | solution.py:19
  88.4 4.2 collective-permute-start.18
  90.7 5.7 %collective-permute-start.19 = (f32[4,1,64,128]{3,2,1,0:T(8,128)S(1)}, f32[4,1,64,128]{3,2,1,0:T(8,128)S(1)}, u32[]{:S(2)}, u32[]{:S(2)}) collective-permute-start(f32[4,1,64,128]{3,2,1,0:T(8,128)S(1)} %get-tuple-element.24), channel_id=1, source_target_pairs={{1,0},{2,1},{3,2},{5,4},{6,5},{7,6},{9,8},{10,9},{11,10},{13,12},{... | collective-permute-start | bytes 393224 | tf_op jit(solution)/shard_map/ppermute | solution.py:19
  96.9 4.1 collective-permute-start.20
  99.1 5.7 %collective-permute-start.21 = (f32[4,1,64,128]{3,2,1,0:T(8,128)S(1)}, f32[4,1,64,128]{3,2,1,0:T(8,128)S(1)}, u32[]{:S(2)}, u32[]{:S(2)}) collective-permute-start(f32[4,1,64,128]{3,2,1,0:T(8,128)S(1)} %get-tuple-element.22), channel_id=1, source_target_pairs={{1,0},{2,1},{3,2},{5,4},{6,5},{7,6},{9,8},{10,9},{11,10},{13,12},{... | collective-permute-start | bytes 393224 | tf_op jit(solution)/shard_map/ppermute | solution.py:19
  105.3 4.1 collective-permute-start.22
  107.5 5.7 %collective-permute-start.23 = (f32[4,1,64,128]{3,2,1,0:T(8,128)S(1)}, f32[4,1,64,128]{3,2,1,0:T(8,128)S(1)}, u32[]{:S(2)}, u32[]{:S(2)}) collective-permute-start(f32[4,1,64,128]{3,2,1,0:T(8,128)S(1)} %get-tuple-element.20), channel_id=1, source_target_pairs={{1,0},{2,1},{3,2},{5,4},{6,5},{7,6},{9,8},{10,9},{11,10},{13,12},{... | collective-permute-start | bytes 393224 | tf_op jit(solution)/shard_map/ppermute | solution.py:19
  113.7 3.9 collective-permute-start.24
  115.6 5.7 %collective-permute-start.25 = (f32[4,1,64,128]{3,2,1,0:T(8,128)S(1)}, f32[4,1,64,128]{3,2,1,0:T(8,128)S(1)}, u32[]{:S(2)}, u32[]{:S(2)}) collective-permute-start(f32[4,1,64,128]{3,2,1,0:T(8,128)S(1)} %get-tuple-element.18), channel_id=1, source_target_pairs={{1,0},{2,1},{3,2},{5,4},{6,5},{7,6},{9,8},{10,9},{11,10},{13,12},{... | collective-permute-start | bytes 393224 | tf_op jit(solution)/shard_map/ppermute | solution.py:19
  123.8 5.7 %collective-permute-start.27 = (f32[4,1,64,128]{3,2,1,0:T(8,128)S(1)}, f32[4,1,64,128]{3,2,1,0:T(8,128)S(1)}, u32[]{:S(2)}, u32[]{:S(2)}) collective-permute-start(f32[4,1,64,128]{3,2,1,0:T(8,128)S(1)} %get-tuple-element.16), channel_id=1, source_target_pairs={{1,0},{2,1},{3,2},{5,4},{6,5},{7,6},{9,8},{10,9},{11,10},{13,12},{... | collective-permute-start | bytes 393224 | tf_op jit(solution)/shard_map/ppermute | solution.py:19
  131.9 5.8 %collective-permute-start.29 = (f32[4,1,64,128]{3,2,1,0:T(8,128)S(1)}, f32[4,1,64,128]{3,2,1,0:T(8,128)S(1)}, u32[]{:S(2)}, u32[]{:S(2)}) collective-permute-start(f32[4,1,64,128]{3,2,1,0:T(8,128)S(1)} %get-tuple-element.14), channel_id=1, source_target_pairs={{1,0},{2,1},{3,2},{5,4},{6,5},{7,6},{9,8},{10,9},{11,10},{13,12},{... | collective-permute-start | bytes 393224 | tf_op jit(solution)/shard_map/ppermute | solution.py:19
  139.1 34.0 %collective-permute-start.30 = (f32[2,4,1,64,128]{4,3,2,1,0:T(8,128)}, f32[2,4,1,64,128]{4,3,2,1,0:T(8,128)}, u32[]{:S(2)}, u32[]{:S(2)}) collective-permute-start(f32[2,4,1,64,128]{4,3,2,1,0:T(8,128)} %get-tuple-element.11), channel_id=1, source_target_pairs={{0,1},{1,2},{2,3},{4,5},{5,6},{6,7},{8,9},{9,10},{10,11},{12,13},{... | collective-permute-start | bytes 786440 | tf_op jit(solution)/shard_map/ppermute | solution.py:16
  141.7 31.4 %collective-permute-start.31 = (f32[2,4,1,64,128]{4,3,2,1,0:T(8,128)}, f32[2,4,1,64,128]{4,3,2,1,0:T(8,128)}, u32[]{:S(2)}, u32[]{:S(2)}) collective-permute-start(f32[2,4,1,64,128]{4,3,2,1,0:T(8,128)} %get-tuple-element.12), channel_id=1, source_target_pairs={{1,0},{2,1},{3,2},{5,4},{6,5},{7,6},{9,8},{10,9},{11,10},{13,12},{... | collective-permute-start | bytes 786440 | tf_op jit(solution)/shard_map/ppermute | solution.py:19
  144.2 46.2 %all-to-all-start = ((f32[4,64,512]{2,0,1:T(4,128)}), f32[4,64,512]{2,0,1:T(4,128)S(1)}, u32[]{:S(2)}, u32[]{:S(2)}) async-start(f32[4,64,512]{2,0,1:T(4,128)} %copy.7), calls=%async_computation | async-start | bytes 1048576 | tf_op jit(solution)/shard_map/all_to_all | solution.py:84
  190.4 23.6 %all-to-all-start.1 = ((f32[4,64,512]{2,0,1:T(4,128)}), f32[4,64,512]{2,0,1:T(4,128)S(1)}, u32[]{:S(2)}, u32[]{:S(2)}) async-start(f32[4,64,512]{2,0,1:T(4,128)} %copy.8), calls=%async_computation.1 | async-start | bytes 1048576 | tf_op jit(solution)/shard_map/all_to_all | solution.py:87
  196.7 264.4 %all-reduce.36.cloned.1.call-start = ((), (), s32[]{:S(2)}) async-start(), calls=%async_computation.3 | async-start | bytes 524288 | tf_op jit(solution)/shard_map/psum | solution.py:99
  (7 other events, 299.0 us)
Sparse Core Ops, SparseCore 0:
  215.7 245.3 all-reduce.35
where the time goes:
time: 499 us; the launch traced here: 498 us
  waiting for transfers between devices  344 us (69%)
  starting transfers between devices  93 us (19%)
  blocking collectives  27.3 us (5%)
  between operations  14.1 us (3%)
  other arithmetic  10.8 us (2%)
  local copies, waits for them, and re-layouts  5.66 us (1%)
    psum x1, waiting for transfers between devices, on_device(): gram = lax.psum(partial_gram, ('dom', 'slab'))  245 us
    ppermute x16, waiting for transfers between devices, with_halo(): lax.ppermute(lax.slice_in_dim(block, 0, width, axis=dim), axis, backward)  57.2 us
    ppermute x16, starting transfers between devices, with_halo(): lax.ppermute(lax.slice_in_dim(block, block.shape[dim] - width, None, axis...  37 us
    all_to_all x1, starting transfers between devices, on_device(): lax.all_to_all(logperm.reshape(particles, -1), 'dom', split_axis=1, conca...  28.9 us
    all_to_all x1, blocking collectives, on_device(): lax.all_to_all(moved, 'dom', split_axis=0, concat_axis=1, tiled=True)  27.3 us
    ppermute x16, starting transfers between devices, with_halo(): lax.ppermute(lax.slice_in_dim(block, 0, width, axis=dim), axis, backward)  20.8 us
    all_to_all x1, waiting for transfers between devices, on_device(): lax.all_to_all(g_flat, 'dom', split_axis=1, concat_axis=0, tiled=True)  16.9 us
    all_to_all x1, waiting for transfers between devices, on_device(): lax.all_to_all(logperm.reshape(particles, -1), 'dom', split_axis=1, conca...  13.7 us
  transfers between devices with their start and end apart: 35, of which 33 were waited for; matrix products, arithmetic and copies ran while one was open for 1% of the time, Pallas kernels for 0%

commit v1 on v0

--- a/solution.py
+++ b/solution.py
@@ -96,7 +96,7 @@
         precision=lax.Precision.HIGHEST,
         preferred_element_type=jnp.float32,
     )
-    gram = lax.psum(partial_gram, ("dom", "slab"))
+    gram = lax.psum(lax.psum(partial_gram, "slab"), "dom")
     step_size = ensemble / (4.0 * (cells + 1))
     mixing = -(step_size / ensemble) * gram + math.sqrt(2.0 * step_size / ensemble) * brownian
     moved = (

time: 499 us -> 473 us (0.948)
  waiting for transfers between devices: 344 us -> 322 us
    psum x1 -> x2, waiting for transfers between devices: 245 us -> 223 us  [on_device(): gram = lax.psum(lax.psum(partial_gram, 'slab'), 'dom')]
  transfers between devices with their start and end apart: 35 -> 36, of which waited for: 33 -> 34; matrix products, arithmetic and copies ran while one was open for 1% -> 1% of each run, Pallas kernels for 0% -> 0%
where the time goes in v1:
time: 473 us; the launch traced here: 472 us
  waiting for transfers between devices  322 us (68%)
  starting transfers between devices  93 us (20%)
  blocking collectives  23.7 us (5%)
  between operations  14.1 us (3%)
  other arithmetic  10.8 us (2%)
  local copies, waits for them, and re-layouts  5.66 us (1%)
    psum x2, waiting for transfers between devices, on_device(): gram = lax.psum(lax.psum(partial_gram, 'slab'), 'dom')  223 us
    ppermute x16, waiting for transfers between devices, with_halo(): lax.ppermute(lax.slice_in_dim(block, 0, width, axis=dim), axis, backward)  57.2 us
    ppermute x16, starting transfers between devices, with_halo(): lax.ppermute(lax.slice_in_dim(block, block.shape[dim] - width, None, axis...  37 us
    all_to_all x1, starting transfers between devices, on_device(): lax.all_to_all(logperm.reshape(particles, -1), 'dom', split_axis=1, conca...  28.9 us
    all_to_all x1, blocking collectives, on_device(): lax.all_to_all(moved, 'dom', split_axis=0, concat_axis=1, tiled=True)  23.7 us
    ppermute x16, starting transfers between devices, with_halo(): lax.ppermute(lax.slice_in_dim(block, 0, width, axis=dim), axis, backward)  20.8 us
    all_to_all x1, waiting for transfers between devices, on_device(): lax.all_to_all(g_flat, 'dom', split_axis=1, concat_axis=0, tiled=True)  16.9 us
    all_to_all x1, waiting for transfers between devices, on_device(): lax.all_to_all(logperm.reshape(particles, -1), 'dom', split_axis=1, conca...  13.7 us
  transfers between devices with their start and end apart: 36, of which 34 were waited for; matrix products, arithmetic and copies ran while one was open for 1% of the time, Pallas kernels for 0%

profile of v1, /device:TPU:1, one launch (start us, length us, event | category | flops | bytes accessed | tf_op | source)
XLA Modules:
  0.0 472.1 jit_solution(8300481808853504410)
XLA Ops:
  7.6 4.0 collective-permute-start
  13.7 3.6 collective-permute-done.1
  18.9 3.2 collective-permute-start.2
  24.1 3.8 collective-permute-done.3
  28.3 2.9 collective-permute-start.4
  33.1 3.8 collective-permute-done.5
  37.3 2.2 collective-permute-start.6
  41.5 3.8 collective-permute-done.7
  49.5 3.8 collective-permute-done.9
  57.6 3.8 collective-permute-done.11
  61.8 2.1 collective-permute-start.12
  66.1 4.1 collective-permute-done.13
  75.3 3.9 collective-permute-done.15
  79.7 2.1 collective-permute-start.16
  84.2 3.8 collective-permute-done.17
  88.4 2.2 collective-permute-start.18
  92.6 3.8 collective-permute-done.19
  96.9 2.2 collective-permute-start.20
  101.0 3.8 collective-permute-done.21
  105.3 2.2 collective-permute-start.22
  109.4 3.8 collective-permute-done.23
  117.5 3.8 collective-permute-done.25
  125.7 3.8 collective-permute-done.27
  133.8 3.9 collective-permute-done.29
  139.1 2.6 collective-permute-start.30
  144.2 28.9 %all-to-all-start = ((f32[4,64,512]{2,0,1:T(4,128)}), f32[4,64,512]{2,0,1:T(4,128)S(1)}, u32[]{:S(2)}, u32[]{:S(2)}) async-start(f32[4,64,512]{2,0,1:T(4,128)} %copy.7), calls=%async_computation | async-start | bytes 1048576 | tf_op jit(solution)/shard_map/all_to_all | solution.py:84
  176.8 13.7 %all-to-all-done = f32[4,64,512]{2,0,1:T(4,128)S(1)} async-done(((f32[4,64,512]{2,0,1:T(4,128)}), f32[4,64,512]{2,0,1:T(4,128)S(1)}, u32[]{:S(2)}, u32[]{:S(2)}) %all-to-all-start) | async-done | bytes 524320 | tf_op jit(solution)/shard_map/all_to_all | solution.py:84
  190.4 6.3 %all-to-all-start.1 = ((f32[4,64,512]{2,0,1:T(4,128)}), f32[4,64,512]{2,0,1:T(4,128)S(1)}, u32[]{:S(2)}, u32[]{:S(2)}) async-start(f32[4,64,512]{2,0,1:T(4,128)} %copy.8), calls=%async_computation.1 | async-start | bytes 1048576 | tf_op jit(solution)/shard_map/all_to_all | solution.py:87
  197.2 16.9 %all-to-all-done.1 = f32[4,64,512]{2,0,1:T(4,128)S(1)} async-done(((f32[4,64,512]{2,0,1:T(4,128)}), f32[4,64,512]{2,0,1:T(4,128)S(1)}, u32[]{:S(2)}, u32[]{:S(2)}) %all-to-all-start.1) | async-done | bytes 524320 | tf_op jit(solution)/shard_map/all_to_all | solution.py:87
  215.6 41.3 %all-reduce.37.cloned.1.call-done = f32[256,256]{1,0:T(8,128)} async-done(((f32[256,256]{1,0:T(8,128)}), f32[256,256]{1,0:T(8,128)}) %all-reduce.37.cloned.1.call-update) | async-done | bytes 262160 | tf_op jit(solution)/shard_map/psum | solution.py:99
  257.2 181.6 %all-reduce.39.cloned.1.call-done = f32[256,256]{1,0:T(8,128)} async-done(((f32[256,256]{1,0:T(8,128)}), f32[256,256]{1,0:T(8,128)}) %all-reduce.39.cloned.1.call-update) | async-done | bytes 262160 | tf_op jit(solution)/shard_map/psum | solution.py:99
  440.6 23.7 %all_to_all.54 = f32[64,4,512]{2,1,0:T(4,128)S(1)} all-to-all(f32[64,4,512]{2,1,0:T(4,128)S(1)} %all_to_all.48), channel_id=1, replica_groups=mesh['dom'=64,'slab'=4] {'dom'}, dimensions={0} | all-to-all | bytes 1048576 | tf_op jit(solution)/shard_map/all_to_all | solution.py:113
  (102 shorter events, 62.8 us)
Async XLA Ops:
  7.6 6.2 %collective-permute-start = (f32[4,1,64,128]{3,2,1,0:T(8,128)S(1)}, f32[4,1,64,128]{3,2,1,0:T(8,128)S(1)}, u32[]{:S(2)}, u32[]{:S(2)}) collective-permute-start(f32[4,1,64,128]{3,2,1,0:T(8,128)S(1)} %get-tuple-element.41), channel_id=1, source_target_pairs={{0,1},{1,2},{2,3},{4,5},{5,6},{6,7},{8,9},{9,10},{10,11},{12,13},{... | collective-permute-start | bytes 393224 | tf_op jit(solution)/shard_map/ppermute | solution.py:16
  11.6 5.7 %collective-permute-start.1 = (f32[4,1,64,128]{3,2,1,0:T(8,128)S(1)}, f32[4,1,64,128]{3,2,1,0:T(8,128)S(1)}, u32[]{:S(2)}, u32[]{:S(2)}) collective-permute-start(f32[4,1,64,128]{3,2,1,0:T(8,128)S(1)} %get-tuple-element.42), channel_id=1, source_target_pairs={{1,0},{2,1},{3,2},{5,4},{6,5},{7,6},{9,8},{10,9},{11,10},{13,12},{... | collective-permute-start | bytes 393224 | tf_op jit(solution)/shard_map/ppermute | solution.py:19
  18.9 5.1 %collective-permute-start.2 = (f32[4,1,64,128]{3,2,1,0:T(8,128)S(1)}, f32[4,1,64,128]{3,2,1,0:T(8,128)S(1)}, u32[]{:S(2)}, u32[]{:S(2)}) collective-permute-start(f32[4,1,64,128]{3,2,1,0:T(8,128)S(1)} %get-tuple-element.39), channel_id=1, source_target_pairs={{0,1},{1,2},{2,3},{4,5},{5,6},{6,7},{8,9},{9,10},{10,11},{12,13},{... | collective-permute-start | bytes 393224 | tf_op jit(solution)/shard_map/ppermute | solution.py:16
  22.2 5.7 %collective-permute-start.3 = (f32[4,1,64,128]{3,2,1,0:T(8,128)S(1)}, f32[4,1,64,128]{3,2,1,0:T(8,128)S(1)}, u32[]{:S(2)}, u32[]{:S(2)}) collective-permute-start(f32[4,1,64,128]{3,2,1,0:T(8,128)S(1)} %get-tuple-element.40), channel_id=1, source_target_pairs={{1,0},{2,1},{3,2},{5,4},{6,5},{7,6},{9,8},{10,9},{11,10},{13,12},{... | collective-permute-start | bytes 393224 | tf_op jit(solution)/shard_map/ppermute | solution.py:19
  28.3 4.8 %collective-permute-start.4 = (f32[4,1,64,128]{3,2,1,0:T(8,128)S(1)}, f32[4,1,64,128]{3,2,1,0:T(8,128)S(1)}, u32[]{:S(2)}, u32[]{:S(2)}) collective-permute-start(f32[4,1,64,128]{3,2,1,0:T(8,128)S(1)} %get-tuple-element.37), channel_id=1, source_target_pairs={{0,1},{1,2},{2,3},{4,5},{5,6},{6,7},{8,9},{9,10},{10,11},{12,13},{... | collective-permute-start | bytes 393224 | tf_op jit(solution)/shard_map/ppermute | solution.py:16
  31.2 5.7 %collective-permute-start.5 = (f32[4,1,64,128]{3,2,1,0:T(8,128)S(1)}, f32[4,1,64,128]{3,2,1,0:T(8,128)S(1)}, u32[]{:S(2)}, u32[]{:S(2)}) collective-permute-start(f32[4,1,64,128]{3,2,1,0:T(8,128)S(1)} %get-tuple-element.38), channel_id=1, source_target_pairs={{1,0},{2,1},{3,2},{5,4},{6,5},{7,6},{9,8},{10,9},{11,10},{13,12},{... | collective-permute-start | bytes 393224 | tf_op jit(solution)/shard_map/ppermute | solution.py:19
  37.3 4.1 collective-permute-start.6
  39.6 5.7 %collective-permute-start.7 = (f32[4,1,64,128]{3,2,1,0:T(8,128)S(1)}, f32[4,1,64,128]{3,2,1,0:T(8,128)S(1)}, u32[]{:S(2)}, u32[]{:S(2)}) collective-permute-start(f32[4,1,64,128]{3,2,1,0:T(8,128)S(1)} %get-tuple-element.36), channel_id=1, source_target_pairs={{1,0},{2,1},{3,2},{5,4},{6,5},{7,6},{9,8},{10,9},{11,10},{13,12},{... | collective-permute-start | bytes 393224 | tf_op jit(solution)/shard_map/ppermute | solution.py:19
  47.6 5.7 %collective-permute-start.9 = (f32[4,1,64,128]{3,2,1,0:T(8,128)S(1)}, f32[4,1,64,128]{3,2,1,0:T(8,128)S(1)}, u32[]{:S(2)}, u32[]{:S(2)}) collective-permute-start(f32[4,1,64,128]{3,2,1,0:T(8,128)S(1)} %get-tuple-element.34), channel_id=1, source_target_pairs={{1,0},{2,1},{3,2},{5,4},{6,5},{7,6},{9,8},{10,9},{11,10},{13,12},{... | collective-permute-start | bytes 393224 | tf_op jit(solution)/shard_map/ppermute | solution.py:19
  53.7 3.9 collective-permute-start.10
  55.7 5.7 %collective-permute-start.11 = (f32[4,1,64,128]{3,2,1,0:T(8,128)S(1)}, f32[4,1,64,128]{3,2,1,0:T(8,128)S(1)}, u32[]{:S(2)}, u32[]{:S(2)}) collective-permute-start(f32[4,1,64,128]{3,2,1,0:T(8,128)S(1)} %get-tuple-element.32), channel_id=1, source_target_pairs={{1,0},{2,1},{3,2},{5,4},{6,5},{7,6},{9,8},{10,9},{11,10},{13,12},{... | collective-permute-start | bytes 393224 | tf_op jit(solution)/shard_map/ppermute | solution.py:19
  61.8 4.3 collective-permute-start.12
  63.9 6.3 %collective-permute-start.13 = (f32[4,1,64,128]{3,2,1,0:T(8,128)S(1)}, f32[4,1,64,128]{3,2,1,0:T(8,128)S(1)}, u32[]{:S(2)}, u32[]{:S(2)}) collective-permute-start(f32[4,1,64,128]{3,2,1,0:T(8,128)S(1)} %get-tuple-element.30), channel_id=1, source_target_pairs={{1,0},{2,1},{3,2},{5,4},{6,5},{7,6},{9,8},{10,9},{11,10},{13,12},{... | collective-permute-start | bytes 393224 | tf_op jit(solution)/shard_map/ppermute | solution.py:19
  70.6 4.7 collective-permute-start.14
  72.3 7.0 %collective-permute-start.15 = (f32[4,1,64,128]{3,2,1,0:T(8,128)S(1)}, f32[4,1,64,128]{3,2,1,0:T(8,128)S(1)}, u32[]{:S(2)}, u32[]{:S(2)}) collective-permute-start(f32[4,1,64,128]{3,2,1,0:T(8,128)S(1)} %get-tuple-element.28), channel_id=1, source_target_pairs={{1,0},{2,1},{3,2},{5,4},{6,5},{7,6},{9,8},{10,9},{11,10},{13,12},{... | collective-permute-start | bytes 393224 | tf_op jit(solution)/shard_map/ppermute | solution.py:19
  79.7 4.4 collective-permute-start.16
  81.9 6.1 %collective-permute-start.17 = (f32[4,1,64,128]{3,2,1,0:T(8,128)S(1)}, f32[4,1,64,128]{3,2,1,0:T(8,128)S(1)}, u32[]{:S(2)}, u32[]{:S(2)}) collective-permute-start(f32[4,1,64,128]{3,2,1,0:T(8,128)S(1)} %get-tuple-element.26), channel_id=1, source_target_pairs={{1,0},{2,1},{3,2},{5,4},{6,5},{7,6},{9,8},{10,9},{11,10},{13,12},{... | collective-permute-start | bytes 393224 | tf_op jit(solution)/shard_map/ppermute | solution.py:19
  88.4 4.2 collective-permute-start.18
  90.7 5.7 %collective-permute-start.19 = (f32[4,1,64,128]{3,2,1,0:T(8,128)S(1)}, f32[4,1,64,128]{3,2,1,0:T(8,128)S(1)}, u32[]{:S(2)}, u32[]{:S(2)}) collective-permute-start(f32[4,1,64,128]{3,2,1,0:T(8,128)S(1)} %get-tuple-element.24), channel_id=1, source_target_pairs={{1,0},{2,1},{3,2},{5,4},{6,5},{7,6},{9,8},{10,9},{11,10},{13,12},{... | collective-permute-start | bytes 393224 | tf_op jit(solution)/shard_map/ppermute | solution.py:19
  96.9 4.1 collective-permute-start.20
  99.1 5.7 %collective-permute-start.21 = (f32[4,1,64,128]{3,2,1,0:T(8,128)S(1)}, f32[4,1,64,128]{3,2,1,0:T(8,128)S(1)}, u32[]{:S(2)}, u32[]{:S(2)}) collective-permute-start(f32[4,1,64,128]{3,2,1,0:T(8,128)S(1)} %get-tuple-element.22), channel_id=1, source_target_pairs={{1,0},{2,1},{3,2},{5,4},{6,5},{7,6},{9,8},{10,9},{11,10},{13,12},{... | collective-permute-start | bytes 393224 | tf_op jit(solution)/shard_map/ppermute | solution.py:19
  105.3 4.1 collective-permute-start.22
  107.5 5.7 %collective-permute-start.23 = (f32[4,1,64,128]{3,2,1,0:T(8,128)S(1)}, f32[4,1,64,128]{3,2,1,0:T(8,128)S(1)}, u32[]{:S(2)}, u32[]{:S(2)}) collective-permute-start(f32[4,1,64,128]{3,2,1,0:T(8,128)S(1)} %get-tuple-element.20), channel_id=1, source_target_pairs={{1,0},{2,1},{3,2},{5,4},{6,5},{7,6},{9,8},{10,9},{11,10},{13,12},{... | collective-permute-start | bytes 393224 | tf_op jit(solution)/shard_map/ppermute | solution.py:19
  115.6 5.7 %collective-permute-start.25 = (f32[4,1,64,128]{3,2,1,0:T(8,128)S(1)}, f32[4,1,64,128]{3,2,1,0:T(8,128)S(1)}, u32[]{:S(2)}, u32[]{:S(2)}) collective-permute-start(f32[4,1,64,128]{3,2,1,0:T(8,128)S(1)} %get-tuple-element.18), channel_id=1, source_target_pairs={{1,0},{2,1},{3,2},{5,4},{6,5},{7,6},{9,8},{10,9},{11,10},{13,12},{... | collective-permute-start | bytes 393224 | tf_op jit(solution)/shard_map/ppermute | solution.py:19
  123.8 5.7 %collective-permute-start.27 = (f32[4,1,64,128]{3,2,1,0:T(8,128)S(1)}, f32[4,1,64,128]{3,2,1,0:T(8,128)S(1)}, u32[]{:S(2)}, u32[]{:S(2)}) collective-permute-start(f32[4,1,64,128]{3,2,1,0:T(8,128)S(1)} %get-tuple-element.16), channel_id=1, source_target_pairs={{1,0},{2,1},{3,2},{5,4},{6,5},{7,6},{9,8},{10,9},{11,10},{13,12},{... | collective-permute-start | bytes 393224 | tf_op jit(solution)/shard_map/ppermute | solution.py:19
  131.9 5.8 %collective-permute-start.29 = (f32[4,1,64,128]{3,2,1,0:T(8,128)S(1)}, f32[4,1,64,128]{3,2,1,0:T(8,128)S(1)}, u32[]{:S(2)}, u32[]{:S(2)}) collective-permute-start(f32[4,1,64,128]{3,2,1,0:T(8,128)S(1)} %get-tuple-element.14), channel_id=1, source_target_pairs={{1,0},{2,1},{3,2},{5,4},{6,5},{7,6},{9,8},{10,9},{11,10},{13,12},{... | collective-permute-start | bytes 393224 | tf_op jit(solution)/shard_map/ppermute | solution.py:19
  139.1 34.0 %collective-permute-start.30 = (f32[2,4,1,64,128]{4,3,2,1,0:T(8,128)}, f32[2,4,1,64,128]{4,3,2,1,0:T(8,128)}, u32[]{:S(2)}, u32[]{:S(2)}) collective-permute-start(f32[2,4,1,64,128]{4,3,2,1,0:T(8,128)} %get-tuple-element.11), channel_id=1, source_target_pairs={{0,1},{1,2},{2,3},{4,5},{5,6},{6,7},{8,9},{9,10},{10,11},{12,13},{... | collective-permute-start | bytes 786440 | tf_op jit(solution)/shard_map/ppermute | solution.py:16
  141.7 31.4 %collective-permute-start.31 = (f32[2,4,1,64,128]{4,3,2,1,0:T(8,128)}, f32[2,4,1,64,128]{4,3,2,1,0:T(8,128)}, u32[]{:S(2)}, u32[]{:S(2)}) collective-permute-start(f32[2,4,1,64,128]{4,3,2,1,0:T(8,128)} %get-tuple-element.12), channel_id=1, source_target_pairs={{1,0},{2,1},{3,2},{5,4},{6,5},{7,6},{9,8},{10,9},{11,10},{13,12},{... | collective-permute-start | bytes 786440 | tf_op jit(solution)/shard_map/ppermute | solution.py:19
  144.2 46.2 %all-to-all-start = ((f32[4,64,512]{2,0,1:T(4,128)}), f32[4,64,512]{2,0,1:T(4,128)S(1)}, u32[]{:S(2)}, u32[]{:S(2)}) async-start(f32[4,64,512]{2,0,1:T(4,128)} %copy.7), calls=%async_computation | async-start | bytes 1048576 | tf_op jit(solution)/shard_map/all_to_all | solution.py:84
  190.4 23.6 %all-to-all-start.1 = ((f32[4,64,512]{2,0,1:T(4,128)}), f32[4,64,512]{2,0,1:T(4,128)S(1)}, u32[]{:S(2)}, u32[]{:S(2)}) async-start(f32[4,64,512]{2,0,1:T(4,128)} %copy.8), calls=%async_computation.1 | async-start | bytes 1048576 | tf_op jit(solution)/shard_map/all_to_all | solution.py:87
  196.7 60.2 %all-reduce.37.cloned.1.call-start = ((), (), s32[]{:S(2)}) async-start(), calls=%async_computation.3 | async-start | bytes 524288 | tf_op jit(solution)/shard_map/psum | solution.py:99
  215.6 223.2 %all-reduce.39.cloned.1.call-start = ((), (), s32[]{:S(2)}) async-start(), calls=%async_computation.4 | async-start | bytes 524288 | tf_op jit(solution)/shard_map/psum | solution.py:99
  (8 other events, 280.5 us)
Sparse Core Ops, SparseCore 0:
  215.7 41.1 all-reduce.36
  260.8 177.8 all-reduce.38
